TPU v7x, 256 devices: a whole 4x4x8 slice. The times are simulated.
256 devices in a mesh: band: 16 (over y, x), lev: 16 (over z, core).
Axes of the slice: x: 4, y: 4, z: 8, core: 2. Of those that a mesh axis runs over, the one named last changes fastest.
Arguments:
- adj_spec: bfloat16 [64, 1280, 2, 1280], P('lev', 'band'), may hold values from -6 to 6
- wave_of_slot: int32 [1280], replicated, may hold values from 0 to 1279, each once
- legendre: bfloat16 [1280, 32, 1280], P('band'), may hold values from -0.15625 to 0.15625
- lat_weight: float32 [32], replicated, may hold values from 0.5 to 1.5
- traj: bfloat16 [64, 64, 5136], P('lev', 'band'), may hold values from -3 to 3
- traj_exp: int32 [64, 64, 4], P('lev', 'band'), may hold values from -2 to 2
- traj_order: int32 [16, 4], P('lev'), may hold values from 0 to 3, each once within a row
- lev_coef: float32 [64], P('lev'), may hold values from 0.02 to 0.2
Outputs:
- adj_out: bfloat16 [64, 1280, 2, 1280], P('lev', 'band')
Inputs may be any that keep to these rules, and one draw needn't show every extreme that they name: `wave_of_slot`: every wavenumber 0 to 1279 is held by exactly one slot. `traj_order`: each row is a permutation of 0 to 3.
All inputs are finite; a program needn't handle non-finite values.
Results may differ from a plain program's by a relative error of at most 0.0085.
Values may be sent and summed in bfloat16 or wider, within the bound.
No kernel may reach another device: no remote copies, remote signals or barrier semaphores. Data moves between devices by JAX's collectives and lax.ppermute only.
A program may use at most 128 MiB of HBM per device.

v0:
```python
import math
import jax
import jax.numpy as jnp
from jax import lax
from jax.sharding import PartitionSpec as P

NBLK = 4
LO = 32


def angles(wave_ids, lon_ids, lon_count):
    phase = lon_ids[:, None] * wave_ids[None, :] % lon_count
    angle = phase.astype(jnp.float32) * (2.0 * math.pi / lon_count)
    return (jnp.cos(angle), jnp.sin(angle))


def quarter_table(wave_ids, width, lon_count):
    steps = -(-width // LO)
    low = angles(wave_ids, jnp.arange(LO, dtype=jnp.int32), lon_count)
    high = angles(wave_ids, jnp.arange(steps, dtype=jnp.int32) * LO, lon_count)
    cos_low, sin_low, cos_high, sin_high = lax.optimization_barrier((*low, *high))
    cos_high, sin_high = (cos_high[:, None], sin_high[:, None])
    cos_all = cos_high * cos_low - sin_high * sin_low
    sin_all = sin_high * cos_low + cos_high * sin_low
    flat = (steps * LO, wave_ids.shape[0])
    cos_all = cos_all.astype(jnp.bfloat16).reshape(flat)
    sin_all = (-sin_all).astype(jnp.bfloat16).reshape(flat)
    return lax.optimization_barrier((cos_all[:width], sin_all[:width]))


def scan_levels(total):
    size, axis = (16, "lev")
    running = total
    step = 1
    while step < size:
        moved = lax.ppermute(
            running.astype(jnp.bfloat16), axis, [(i, i + step) for i in range(size - step)]
        )
        running = running + moved.astype(jnp.float32)
        step *= 2
    return lax.ppermute(
        running.astype(jnp.bfloat16), axis, [(i, i + 1) for i in range(size - 1)]
    ).astype(jnp.float32)


def body(adj_spec, wave_of_slot, legendre, lat_weight, traj, traj_exp, traj_order, lev_coef):
    bf16, f32 = (jnp.bfloat16, jnp.float32)
    highest = lax.Precision.HIGHEST
    levels, slots, _, degrees = adj_spec.shape
    lat_rows, lon_count = traj.shape[1:]
    width = lon_count // NBLK
    norm_scale = 1.0 / math.sqrt(degrees)
    waves_here = lax.dynamic_slice_in_dim(wave_of_slot, lax.axis_index("band") * slots, slots)
    degree_ids = jnp.arange(degrees, dtype=jnp.int32)
    valid = degree_ids[None, :] < (degrees - waves_here)[:, None]
    masked = jnp.where(valid[None, :, None, :], adj_spec, jnp.zeros_like(adj_spec))
    sign = jnp.where(degree_ids % 2 == 0, 1.0, -1.0).astype(bf16)
    stacked = jnp.stack([masked, masked * sign], axis=3)
    side = jnp.einsum("lscej,shj->lsche", stacked, legendre, preferred_element_type=f32)
    weight_q = jnp.repeat(lat_weight, 2)
    fourier = (side.reshape(levels, slots, 2, -1) * weight_q).astype(bf16)
    fourier = lax.all_to_all(fourier, "band", split_axis=3, concat_axis=1, tiled=True)
    total = jnp.sum(fourier.astype(f32), axis=0)
    carry = scan_levels(total)
    cos_t, sin_t = quarter_table(wave_of_slot, width, lon_count)
    turn = jnp.arange(NBLK, dtype=jnp.int32)[:, None] * wave_of_slot[None, :] % 4
    cos_b = jnp.where(turn == 0, 1.0, jnp.where(turn == 2, -1.0, 0.0))
    sin_b = jnp.where(turn == 1, 1.0, jnp.where(turn == 3, -1.0, 0.0))

    def to_grid(rows):
        first, second = (rows[:, None, :, 0], rows[:, None, :, 1])
        first, second = (jnp.moveaxis(first, 2, 3), jnp.moveaxis(second, 2, 3))
        cb, sb = (cos_b[None, :, None, :], sin_b[None, :, None, :])
        with_cos = (first * cb - second * sb).astype(bf16)
        with_sin = (first * sb + second * cb).astype(bf16)
        out = jnp.einsum("lbqs,ks->lbqk", with_cos, cos_t, preferred_element_type=f32)
        out = out + jnp.einsum("lbqs,ks->lbqk", with_sin, sin_t, preferred_element_type=f32)
        return out * norm_scale

    grid = to_grid(fourier.astype(f32))
    group = to_grid(carry[None])
    running = jnp.cumsum(grid, axis=0)
    above = jnp.concatenate([jnp.zeros_like(grid[:1]), running[:-1]], axis=0) + group
    order = jnp.arange(levels, dtype=jnp.int32)
    select = (traj_order[0][None, :] == order[:, None]).astype(f32)
    scaled = traj.astype(f32).reshape(levels, lat_rows, NBLK, width)
    scaled = scaled * jnp.exp2(traj_exp.astype(f32))[..., None]
    ordered = jnp.einsum("ir,rqbk->ibqk", select, scaled, precision=highest)
    forcing = (1.0 + jnp.tanh(ordered)) * (grid + lev_coef[:, None, None, None] * above)
    forcing = forcing.astype(bf16)
    by_cos = jnp.einsum("lbqk,ks->lbqs", forcing, cos_t, preferred_element_type=f32)
    by_sin = jnp.einsum("lbqk,ks->lbqs", forcing, sin_t, preferred_element_type=f32)
    cb, sb = (cos_b[None, :, None, :], sin_b[None, :, None, :])
    first = jnp.sum(by_cos * cb + by_sin * sb, axis=1) * norm_scale
    second = jnp.sum(by_sin * cb - by_cos * sb, axis=1) * norm_scale
    analysis = jnp.stack([first, second], axis=1)
    halves = analysis.reshape(levels, 2, lat_rows // 2, 2, -1)
    sym = halves[:, :, :, 0] + halves[:, :, :, 1]
    anti = halves[:, :, :, 0] - halves[:, :, :, 1]
    sides = jnp.stack([sym, anti], axis=2).astype(bf16)
    sides = lax.all_to_all(sides, "band", split_axis=4, concat_axis=3, tiled=True)
    both = jnp.einsum("lcehs,shj->lsecj", sides, legendre, preferred_element_type=f32)
    result = jnp.where(degree_ids % 2 == 0, both[:, :, 0], both[:, :, 1])
    return jnp.where(valid[None, :, None, :], result, 0.0).astype(bf16)


def solution(mesh):
    return jax.shard_map(
        body,
        mesh=mesh,
        in_specs=(
            P("lev", "band", None, None),
            P(),
            P("band", None, None),
            P(),
            P("lev", "band", None),
            P("lev", "band", None),
            P("lev", None),
            P("lev"),
        ),
        out_specs=P("lev", "band", None, None),
        check_vma=False,
    )
```

profile of v0, /device:TPU:97, one launch (start us, length us, event | category | flops | bytes accessed | tf_op | source)
XLA Modules:
  0.0 117.2 jit_solution(4242895154096673147)
XLA Ops:
  1.5 3.5 %fusion.46 = (bf16[4,80,2,1,1280]{4,0,3,2,1:T(4,128)(2,1)S(1)}, bf16[4,80,2,1,1280]{4,0,3,2,1:T(4,128)(2,1)S(1)}) fusion(bf16[4,80,2,1280]{3,2,1,0:T(2,128)(2,1)} %param.8, pred[80,1280]{1,0:T(8,128)(4,1)S(1)} %iota_compare_fusion, bf16[1280]{0:T(1024)(128)(2,1)S(1)} %select_convert_fusion), kind=kLoop, calls=%fused_computation.39 | loop fusion | flops 1638400 | bytes 5020160 | tf_op jit(solution)/shard_map/stack | solution.py:58
  5.1 6.2 %fusion.41 = f32[4,80,2,32,2]{3,0,4,2,1:T(4,128)S(1)} fusion(bf16[80,32,1280]{2,1,0:T(8,128)(2,1)} %param.10, bf16[4,80,2,1,1280]{4,0,3,2,1:T(4,128)(2,1)S(1)} %get-tuple-element.20, bf16[4,80,2,1,1280]{4,0,3,2,1:T(4,128)(2,1)S(1)} %get-tuple-element.19), kind=kOutput, calls=%fused_computation.38 | convolution fusion | flops 111411200 | bytes 9994240 | tf_op jit(solution)/shard_map/lscej,shj->lsche/dot_general | solution.py:59
  12.6 6.8 %all-to-all-start = ((bf16[4,80,2,64]{1,2,0,3:T(2,128)(2,1)}), bf16[4,80,2,64]{1,2,0,3:T(2,128)(2,1)S(1)}, u32[]{:S(2)}, u32[]{:S(2)}) async-start(bf16[4,80,2,64]{1,2,0,3:T(2,128)(2,1)} %copy.62), calls=%async_computation | async-start | bytes 262144 | tf_op jit(solution)/shard_map/all_to_all | solution.py:62
  21.2 2.5 %negate_convert_fusion = (bf16[41,32,1280]{2,1,0:T(8,128)(2,1)S(1)}, bf16[41,32,1280]{2,1,0:T(8,128)(2,1)S(1)}) fusion(f32[32,1280]{1,0:T(8,128)S(1)} %get-tuple-element.14, f32[41,1280]{1,0:T(8,128)S(1)} %get-tuple-element.13, f32[32,1280]{1,0:T(8,128)S(1)} %get-tuple-element.12, f32[41,1280]{1,0:T(8,128)S(1)} %get-tuple-element.11), kind=kLoop, calls=%fused_computation | loop fusion | flops 15114240 | bytes 7464960 | tf_op jit(solution)/shard_map/convert_element_type | solution.py:27
  23.8 1.9 %slice.48 = bf16[1284,1280]{1,0:T(8,128)(2,1)} slice(bf16[1312,1280]{1,0:T(8,128)(2,1)S(1)} %bitcast.135), slice={[0:1284], [0:1280]} | slice | bytes 6574080 | tf_op jit(solution)/shard_map/slice | solution.py:28
  25.9 1.9 %reshape.192 = f32[4,4,4,1284]{3,2,1,0:T(4,128)} reshape(bf16[4,4,5136]{2,1,0:T(4,128)(2,1)} %param.12) | data formatting | bytes 493056 | tf_op jit(solution)/shard_map/reshape | solution.py:86
  30.1 5.6 %collective-permute-start = (bf16[1280,2,4]{0,2,1:T(4,128)(2,1)S(1)}, bf16[1280,2,4]{0,2,1:T(4,128)(2,1)S(1)}, u32[]{:S(2)}, u32[]{:S(2)}) collective-permute-start(bf16[1280,2,4]{0,2,1:T(4,128)(2,1)S(1)} %convert_element_type.122), channel_id=1, source_target_pairs={{0,1},{1,2},{2,3},{3,4},{4,5},{5,6},{6,7},{7,8},{8,9},{9,10},{10,1... | collective-permute-start | bytes 61448 | tf_op jit(solution)/shard_map/ppermute | solution.py:36
  36.5 1.8 %reshape.193 = f32[4,1280,2,4]{1,3,2,0:T(4,128)} reshape(f32[4,16,80,2,4]{2,1,4,3,0:T(8,128)} %copy.64) | data formatting | bytes 327680 | tf_op jit(solution)/shard_map/convert_element_type | solution.py:80
  38.3 2.6 %collective-permute-start.1 = (bf16[1280,2,4]{0,2,1:T(4,128)(2,1)S(1)}, bf16[1280,2,4]{0,2,1:T(4,128)(2,1)S(1)}, u32[]{:S(2)}, u32[]{:S(2)}) collective-permute-start(bf16[1280,2,4]{0,2,1:T(4,128)(2,1)S(1)} %fusion.78), channel_id=1, source_target_pairs={{0,2},{1,3},{2,4},{3,5},{4,6},{5,7},{6,8},{7,9},{8,10},{9,11},{10,... | collective-permute-start | bytes 61448 | tf_op jit(solution)/shard_map/ppermute | solution.py:36
  42.9 3.1 %collective-permute-start.2 = (bf16[1280,2,4]{0,2,1:T(4,128)(2,1)S(1)}, bf16[1280,2,4]{0,2,1:T(4,128)(2,1)S(1)}, u32[]{:S(2)}, u32[]{:S(2)}) collective-permute-start(bf16[1280,2,4]{0,2,1:T(4,128)(2,1)S(1)} %fusion.89), channel_id=1, source_target_pairs={{0,4},{1,5},{2,6},{3,7},{4,8},{5,9},{6,10},{7,11},{8,12},{9,13},{1... | collective-permute-start | bytes 61448 | tf_op jit(solution)/shard_map/ppermute | solution.py:36
  46.2 2.1 %collective-permute-done.2 = bf16[1280,2,4]{0,2,1:T(4,128)(2,1)S(1)} collective-permute-done((bf16[1280,2,4]{0,2,1:T(4,128)(2,1)S(1)}, bf16[1280,2,4]{0,2,1:T(4,128)(2,1)S(1)}, u32[]{:S(2)}, u32[]{:S(2)}) %collective-permute-start.2) | collective-permute-done | bytes 20512 | tf_op jit(solution)/shard_map/ppermute | solution.py:36
  48.3 3.3 %collective-permute-start.3 = (bf16[1280,2,4]{0,2,1:T(4,128)(2,1)S(1)}, bf16[1280,2,4]{0,2,1:T(4,128)(2,1)S(1)}, u32[]{:S(2)}, u32[]{:S(2)}) collective-permute-start(bf16[1280,2,4]{0,2,1:T(4,128)(2,1)S(1)} %fusion.79), channel_id=1, source_target_pairs={{0,8},{1,9},{2,10},{3,11},{4,12},{5,13},{6,14},{7,15},{16,24},{17,... | collective-permute-start | bytes 61448 | tf_op jit(solution)/shard_map/ppermute | solution.py:36
  52.9 13.7 %collective-permute-start.4 = (bf16[1280,2,4]{0,2,1:T(4,128)(2,1)S(1)}, bf16[1280,2,4]{0,2,1:T(4,128)(2,1)S(1)}, u32[]{:S(2)}, u32[]{:S(2)}) collective-permute-start(bf16[1280,2,4]{0,2,1:T(4,128)(2,1)S(1)} %add_convert_fusion.4), channel_id=1, source_target_pairs={{0,1},{1,2},{2,3},{3,4},{4,5},{5,6},{6,7},{7,8},{8,9},{9,10},{10,1... | collective-permute-start | bytes 61448 | tf_op jit(solution)/shard_map/ppermute | solution.py:41
  66.6 2.0 %fusion.28 = f32[4,4,4,1284]{3,0,1,2:T(4,128)} fusion(f32[4,4,4,1284]{3,0,1,2:T(4,128)S(1)} %fusion.15, bf16[1284,1280]{1,0:T(8,128)(2,1)S(1)} %copy-done, bf16[4,4,4,1280]{3,2,1,0:T(4,128)(2,1)S(1)} %get-tuple-element.23), kind=kOutput, calls=%fused_computation.28 | convolution fusion | flops 210534912 | bytes 4108288 | tf_op jit(solution)/shard_map/lbqs,ks->lbqk/dot_general | solution.py:76
  68.6 2.2 %reduce_window_sum.11 = f32[4,4,4,1284]{3,0,1,2:T(4,128)} reduce-window(f32[4,4,4,1284]{3,0,1,2:T(4,128)} %fusion.28, f32[]{:T(128)} %constant.88.clone.1), window={size=4x1x1x1 pad=3_0x0_0x0_0x0_0}, to_apply=%region_0.1 | reduce-window | flops 246528 | bytes 657412 | tf_op jit(solution)/shard_map/jit(cumsum)/reduce_window_sum | solution.py:82
  76.6 3.5 %copy.75 = bf16[4,2,2,2,1280]{0,3,1,2,4:T(2,128)(2,1)S(1)} copy(bf16[4,2,2,2,1280]{4,0,3,1,2:T(4,128)(2,1)S(1)} %pad_maximum_fusion.1) | data formatting | bytes 163840 | tf_op jit(solution)/shard_map/stack | solution.py:100
  80.2 5.7 %reshape.202 = bf16[16,2,1280]{2,1,0:T(2,128)(2,1)} reshape(bf16[1280,2,2,2,4]{4,3,2,1,0:T(2,128)(2,1)S(1)} %bitcast.136) | data formatting | bytes 163840
  85.9 6.9 %all-to-all-start.1 = ((bf16[16,2,1280]{2,1,0:T(2,128)(2,1)}), bf16[16,2,1280]{2,1,0:T(2,128)(2,1)S(1)}, u32[]{:S(2)}, u32[]{:S(2)}) async-start(bf16[16,2,1280]{2,1,0:T(2,128)(2,1)} %reshape.202), calls=%async_computation.1 | async-start | bytes 163840 | tf_op jit(solution)/shard_map/all_to_all | solution.py:101
  92.8 6.6 %all-to-all-done.1 = bf16[16,2,1280]{2,1,0:T(2,128)(2,1)S(1)} async-done(((bf16[16,2,1280]{2,1,0:T(2,128)(2,1)}), bf16[16,2,1280]{2,1,0:T(2,128)(2,1)S(1)}, u32[]{:S(2)}, u32[]{:S(2)}) %all-to-all-start.1) | async-done | bytes 81952 | tf_op jit(solution)/shard_map/all_to_all | solution.py:101
  99.4 5.6 %reshape.203 = bf16[1280,2,2,2,4]{4,3,2,1,0:T(2,128)(2,1)S(1)} reshape(bf16[16,2,1280]{2,1,0:T(2,128)(2,1)S(1)} %all-to-all-done.1) | data formatting | bytes 163840
  105.0 3.6 %copy.93 = bf16[4,2,2,2,16,80]{5,4,3,2,1,0:T(8,128)(2,1)S(1)} copy(bf16[4,2,2,2,16,80]{0,3,1,2,5,4:T(2,128)(2,1)S(1)} %bitcast.137) | data formatting | bytes 163840 | tf_op jit(solution)/shard_map/all_to_all | solution.py:101
  109.0 4.2 %fusion.4 = bf16[4,80,2,2,1280]{4,0,3,1,2:T(4,128)(2,1)S(1)} fusion(bf16[4,2,2,32,80]{3,0,1,4,2:T(4,128)(2,1)S(1)} %copy.89, bf16[80,32,1280]{2,1,0:T(8,128)(2,1)} %param.10), kind=kOutput, calls=%fused_computation.6 | convolution fusion | flops 104857600 | bytes 9912320 | tf_op jit(solution)/shard_map/lcehs,shj->lsecj/dot_general | solution.py:102
  113.2 1.6 %fusion.21 = bf16[4,80,2,1280]{3,0,2,1:T(4,128)(2,1)S(1)} fusion(bf16[4,80,2,2,1280]{4,0,3,1,2:T(4,128)(2,1)S(1)} %fusion.4, pred[1280]{0:T(1024)(128)(4,1)S(1)} %fusion.81, pred[80,1280]{1,0:T(8,128)(4,1)S(1)} %copy-done.3), kind=kLoop, calls=%fused_computation.22 | loop fusion | flops 1638400 | bytes 5018880 | tf_op jit(solution)/shard_map/convert_element_type | solution.py:104
  114.8 2.4 %copy.80 = bf16[4,80,2,1280]{3,2,1,0:T(2,128)(2,1)} copy(bf16[4,80,2,1280]{3,0,2,1:T(4,128)(2,1)S(1)} %fusion.21) | data formatting | bytes 3276800 | tf_op jit(solution)/shard_map/convert_element_type | solution.py:104
  (75 shorter events, 17.4 us)
Async XLA Ops:
  0.9 0.6 copy-start.2
  5.1 6.5 %copy-start.10 = (f32[32]{0:T(128)S(1)}, f32[32]{0:T(128)}, u32[]{:S(2)}) copy-start(f32[32]{0:T(128)} %param.11) | copy-start | bytes 388
  5.1 14.3 %copy-start.7 = (s32[1280]{0:T(1024)S(1)}, s32[1280]{0:T(1024)}, u32[]{:S(2)}) copy-start(s32[1280]{0:T(1024)} %param.9) | copy-start | bytes 15364
  12.6 15.9 %all-to-all-start = ((bf16[4,80,2,64]{1,2,0,3:T(2,128)(2,1)}), bf16[4,80,2,64]{1,2,0,3:T(2,128)(2,1)S(1)}, u32[]{:S(2)}, u32[]{:S(2)}) async-start(bf16[4,80,2,64]{1,2,0,3:T(2,128)(2,1)} %copy.62), calls=%async_computation | async-start | bytes 262144 | tf_op jit(solution)/shard_map/all_to_all | solution.py:62
  21.2 2.5 %copy-start.8 = (s32[4,4,4]{2,1,0:T(4,128)S(1)}, s32[4,4,4]{2,1,0:T(4,128)}, u32[]{:S(2)}) copy-start(s32[4,4,4]{2,1,0:T(4,128)} %param.13) | copy-start | bytes 772
  30.1 8.2 %collective-permute-start = (bf16[1280,2,4]{0,2,1:T(4,128)(2,1)S(1)}, bf16[1280,2,4]{0,2,1:T(4,128)(2,1)S(1)}, u32[]{:S(2)}, u32[]{:S(2)}) collective-permute-start(bf16[1280,2,4]{0,2,1:T(4,128)(2,1)S(1)} %convert_element_type.122), channel_id=1, source_target_pairs={{0,1},{1,2},{2,3},{3,4},{4,5},{5,6},{6,7},{7,8},{8,9},{9,10},{10,1... | collective-permute-start | bytes 61448 | tf_op jit(solution)/shard_map/ppermute | solution.py:36
  38.3 4.5 %collective-permute-start.1 = (bf16[1280,2,4]{0,2,1:T(4,128)(2,1)S(1)}, bf16[1280,2,4]{0,2,1:T(4,128)(2,1)S(1)}, u32[]{:S(2)}, u32[]{:S(2)}) collective-permute-start(bf16[1280,2,4]{0,2,1:T(4,128)(2,1)S(1)} %fusion.78), channel_id=1, source_target_pairs={{0,2},{1,3},{2,4},{3,5},{4,6},{5,7},{6,8},{7,9},{8,10},{9,11},{10,... | collective-permute-start | bytes 61448 | tf_op jit(solution)/shard_map/ppermute | solution.py:36
  42.9 5.4 %collective-permute-start.2 = (bf16[1280,2,4]{0,2,1:T(4,128)(2,1)S(1)}, bf16[1280,2,4]{0,2,1:T(4,128)(2,1)S(1)}, u32[]{:S(2)}, u32[]{:S(2)}) collective-permute-start(bf16[1280,2,4]{0,2,1:T(4,128)(2,1)S(1)} %fusion.89), channel_id=1, source_target_pairs={{0,4},{1,5},{2,6},{3,7},{4,8},{5,9},{6,10},{7,11},{8,12},{9,13},{1... | collective-permute-start | bytes 61448 | tf_op jit(solution)/shard_map/ppermute | solution.py:36
  46.2 20.4 %copy-start = (bf16[1284,1280]{1,0:T(8,128)(2,1)S(1)}, bf16[1284,1280]{1,0:T(8,128)(2,1)}, u32[]{:S(2)}) copy-start(bf16[1284,1280]{1,0:T(8,128)(2,1)} %slice.48) | copy-start | bytes 9861124
  48.3 4.5 %collective-permute-start.3 = (bf16[1280,2,4]{0,2,1:T(4,128)(2,1)S(1)}, bf16[1280,2,4]{0,2,1:T(4,128)(2,1)S(1)}, u32[]{:S(2)}, u32[]{:S(2)}) collective-permute-start(bf16[1280,2,4]{0,2,1:T(4,128)(2,1)S(1)} %fusion.79), channel_id=1, source_target_pairs={{0,8},{1,9},{2,10},{3,11},{4,12},{5,13},{6,14},{7,15},{16,24},{17,... | collective-permute-start | bytes 61448 | tf_op jit(solution)/shard_map/ppermute | solution.py:36
  52.9 17.9 %collective-permute-start.4 = (bf16[1280,2,4]{0,2,1:T(4,128)(2,1)S(1)}, bf16[1280,2,4]{0,2,1:T(4,128)(2,1)S(1)}, u32[]{:S(2)}, u32[]{:S(2)}) collective-permute-start(bf16[1280,2,4]{0,2,1:T(4,128)(2,1)S(1)} %add_convert_fusion.4), channel_id=1, source_target_pairs={{0,1},{1,2},{2,3},{3,4},{4,5},{5,6},{6,7},{7,8},{8,9},{9,10},{10,1... | collective-permute-start | bytes 61448 | tf_op jit(solution)/shard_map/ppermute | solution.py:41
  70.8 1.9 %copy-start.1 = (bf16[1284,1280]{1,0:T(8,128)(2,1)S(1)}, bf16[1284,1280]{1,0:T(8,128)(2,1)}, u32[]{:S(2)}) copy-start(bf16[1284,1280]{1,0:T(8,128)(2,1)} %slice.48) | copy-start | bytes 9861124
  70.8 3.0 %copy-start.4 = (f32[4,4,4,1284]{3,2,1,0:T(4,128)S(1)}, f32[4,4,4,1284]{3,2,1,0:T(4,128)}, u32[]{:S(2)}) copy-start(f32[4,4,4,1284]{3,2,1,0:T(4,128)} %reshape.192) | copy-start | bytes 986116
  70.8 3.0 %copy-start.5 = (f32[4,4,4,1284]{3,0,1,2:T(4,128)S(1)}, f32[4,4,4,1284]{3,0,1,2:T(4,128)}, u32[]{:S(2)}) copy-start(f32[4,4,4,1284]{3,0,1,2:T(4,128)} %fusion.28) | copy-start | bytes 986116
  70.8 3.0 %copy-start.6 = (f32[4,4,4,1284]{3,0,1,2:T(4,128)S(1)}, f32[4,4,4,1284]{3,0,1,2:T(4,128)}, u32[]{:S(2)}) copy-start(f32[4,4,4,1284]{3,0,1,2:T(4,128)} %reduce_window_sum.11) | copy-start | bytes 986116
  70.9 3.0 %copy-start.9 = (f32[4,4,4]{0,2,1:T(4,128)S(1)}, f32[4,4,4]{0,2,1:T(4,128)}, u32[]{:S(2)}) copy-start(f32[4,4,4]{0,2,1:T(4,128)} %copy.57) | copy-start | bytes 772
  70.9 3.0 %copy-start.11 = (f32[4]{0:T(128)S(1)}, f32[4]{0:T(128)}, u32[]{:S(2)}) copy-start(f32[4]{0:T(128)} %param.15) | copy-start | bytes 52
  70.9 3.0 %copy-start.12 = (s32[1,4]{1,0:T(1,128)S(1)}, s32[1,4]{1,0:T(1,128)}, u32[]{:S(2)}) copy-start(s32[1,4]{1,0:T(1,128)} %param.14) | copy-start | bytes 52
  85.9 13.5 %all-to-all-start.1 = ((bf16[16,2,1280]{2,1,0:T(2,128)(2,1)}), bf16[16,2,1280]{2,1,0:T(2,128)(2,1)S(1)}, u32[]{:S(2)}, u32[]{:S(2)}) async-start(bf16[16,2,1280]{2,1,0:T(2,128)(2,1)} %reshape.202), calls=%async_computation.1 | async-start | bytes 163840 | tf_op jit(solution)/shard_map/all_to_all | solution.py:101
  109.0 4.2 %copy-start.3 = (pred[80,1280]{1,0:T(8,128)(4,1)S(1)}, pred[80,1280]{1,0:T(8,128)(4,1)}, u32[]{:S(2)}) copy-start(pred[80,1280]{1,0:T(8,128)(4,1)} %copy-done.2) | copy-start | bytes 307204
where the time goes:
time: 118 us; the launch traced here: 117 us
  starting transfers between devices  42 us (36%)
  local copies, waits for them, and re-layouts  33.8 us (29%)
  matrix products  18.2 us (15%)
  other arithmetic  13.1 us (11%)
  waiting for transfers between devices  9.62 us (8%)
    ppermute x4, starting transfers between devices, scan_levels(): lax.ppermute(running.astype(jnp.bfloat16), axis, [(i, i + step) for i in...  14.6 us
    ppermute x1, starting transfers between devices, scan_levels(): lax.ppermute(running.astype(jnp.bfloat16), axis, [(i, i + 1) for i in ran...  13.7 us
    unnamed x28, local copies, waits for them, and re-layouts  12.8 us
    all_to_all x1, starting transfers between devices, body(): lax.all_to_all(sides, 'band', split_axis=4, concat_axis=3, tiled=True)  6.95 us
    all_to_all x1, starting transfers between devices, body(): lax.all_to_all(fourier, 'band', split_axis=3, concat_axis=1, tiled=True)  6.75 us
    all_to_all x1, waiting for transfers between devices, body(): lax.all_to_all(sides, 'band', split_axis=4, concat_axis=3, tiled=True)  6.56 us
    dot_general x1, matrix products, body(): jnp.einsum('lscej,shj->lsche', stacked, legendre, preferred_element_type=...  6.16 us
    dot_general x1, matrix products, body(): jnp.einsum('lcehs,shj->lsecj', sides, legendre, preferred_element_type=f32)  4.15 us
  transfers between devices with their start and end apart: 7, of which 3 were waited for; matrix products, arithmetic and copies ran while one was open for 15% of the time, Pallas kernels for 0%

commit v1 on v0

--- a/solution.py
+++ b/solution.py
@@ -98,7 +98,9 @@
     sym = halves[:, :, :, 0] + halves[:, :, :, 1]
     anti = halves[:, :, :, 0] - halves[:, :, :, 1]
     sides = jnp.stack([sym, anti], axis=2).astype(bf16)
-    sides = lax.all_to_all(sides, "band", split_axis=4, concat_axis=3, tiled=True)
+    pieces = jnp.split(sides, lax.axis_size("band"), axis=4)
+    received = lax.all_to_all(jnp.stack(pieces), "band", 0, 0)
+    sides = jnp.concatenate(received, axis=3)
     both = jnp.einsum("lcehs,shj->lsecj", sides, legendre, preferred_element_type=f32)
     result = jnp.where(degree_ids % 2 == 0, both[:, :, 0], both[:, :, 1])
     return jnp.where(valid[None, :, None, :], result, 0.0).astype(bf16)

time: 118 us -> 110 us (0.932)
  local copies, waits for them, and re-layouts: 33.8 us -> 15.4 us
  other arithmetic: 13.1 us -> 23.7 us
    unnamed x28 -> x26, local copies, waits for them, and re-layouts: 12.8 us -> 1.48 us
    unnamed x0 -> x15, other arithmetic: none -> 9.99 us
    all_to_all x3 -> x0, local copies, waits for them, and re-layouts: 3.95 us -> none  [body(): lax.all_to_all(sides, 'band', split_axis=4, concat_axis=3, tiled=True)]
    another operation x1 -> x0, local copies, waits for them, and re-layouts: 3.52 us -> none  [body(): sides = jnp.stack([sym, anti], axis=2).astype(bf16)]
  transfers between devices with their start and end apart: 7 -> 7, of which waited for: 3 -> 3; matrix products, arithmetic and copies ran while one was open for 15% -> 17% of each run, Pallas kernels for 0% -> 0%
where the time goes in v1:
time: 110 us
  starting transfers between devices  42 us (38%)
  other arithmetic  23.7 us (22%)
  matrix products  18.2 us (17%)
  local copies, waits for them, and re-layouts  15.4 us (14%)
  waiting for transfers between devices  9.89 us (9%)
    ppermute x4, starting transfers between devices, scan_levels(): lax.ppermute(running.astype(jnp.bfloat16), axis, [(i, i + step) for i in...  14.6 us
    ppermute x1, starting transfers between devices, scan_levels(): lax.ppermute(running.astype(jnp.bfloat16), axis, [(i, i + 1) for i in ran...  13.7 us
    unnamed x15, other arithmetic  9.99 us
    all_to_all x1, starting transfers between devices, body(): received = lax.all_to_all(jnp.stack(pieces), 'band', 0, 0)  6.93 us
    all_to_all x1, waiting for transfers between devices, body(): received = lax.all_to_all(jnp.stack(pieces), 'band', 0, 0)  6.83 us
    all_to_all x1, starting transfers between devices, body(): lax.all_to_all(fourier, 'band', split_axis=3, concat_axis=1, tiled=True)  6.75 us
    dot_general x1, matrix products, body(): jnp.einsum('lscej,shj->lsche', stacked, legendre, preferred_element_type=...  6.16 us
    dot_general x1, matrix products, body(): jnp.einsum('lcehs,shj->lsecj', sides, legendre, preferred_element_type=f32)  4.15 us
  transfers between devices with their start and end apart: 7, of which 3 were waited for; matrix products, arithmetic and copies ran while one was open for 17% of the time, Pallas kernels for 0%

profile of v1, /device:TPU:97, one launch (start us, length us, event | category | flops | bytes accessed | tf_op | source)
XLA Modules:
  0.0 109.6 jit_solution(15615530718381744761)
XLA Ops:
  1.5 3.5 %fusion.46 = (bf16[4,80,2,1,1280]{4,0,3,2,1:T(4,128)(2,1)S(1)}, bf16[4,80,2,1,1280]{4,0,3,2,1:T(4,128)(2,1)S(1)}) fusion(bf16[4,80,2,1280]{3,2,1,0:T(2,128)(2,1)} %param.8, pred[80,1280]{1,0:T(8,128)(4,1)S(1)} %iota_compare_fusion, bf16[1280]{0:T(1024)(128)(2,1)S(1)} %select_convert_fusion), kind=kLoop, calls=%fused_computation.39 | loop fusion | flops 1638400 | bytes 5020160 | tf_op jit(solution)/shard_map/stack | solution.py:58
  5.1 6.2 %fusion.41 = f32[4,80,2,32,2]{3,0,4,2,1:T(4,128)S(1)} fusion(bf16[80,32,1280]{2,1,0:T(8,128)(2,1)} %param.10, bf16[4,80,2,1,1280]{4,0,3,2,1:T(4,128)(2,1)S(1)} %get-tuple-element.20, bf16[4,80,2,1,1280]{4,0,3,2,1:T(4,128)(2,1)S(1)} %get-tuple-element.19), kind=kOutput, calls=%fused_computation.38 | convolution fusion | flops 111411200 | bytes 9994240 | tf_op jit(solution)/shard_map/lscej,shj->lsche/dot_general | solution.py:59
  12.6 6.8 %all-to-all-start = ((bf16[4,80,2,64]{1,2,0,3:T(2,128)(2,1)}), bf16[4,80,2,64]{1,2,0,3:T(2,128)(2,1)S(1)}, u32[]{:S(2)}, u32[]{:S(2)}) async-start(bf16[4,80,2,64]{1,2,0,3:T(2,128)(2,1)} %copy.81), calls=%async_computation | async-start | bytes 262144 | tf_op jit(solution)/shard_map/all_to_all | solution.py:62
  20.1 1.1 fusion.51
  21.2 2.5 %negate_convert_fusion = (bf16[41,32,1280]{2,1,0:T(8,128)(2,1)S(1)}, bf16[41,32,1280]{2,1,0:T(8,128)(2,1)S(1)}) fusion(f32[32,1280]{1,0:T(8,128)S(1)} %get-tuple-element.14, f32[41,1280]{1,0:T(8,128)S(1)} %get-tuple-element.13, f32[32,1280]{1,0:T(8,128)S(1)} %get-tuple-element.12, f32[41,1280]{1,0:T(8,128)S(1)} %get-tuple-element.11), kind=kLoop, calls=%fused_computation | loop fusion | flops 15114240 | bytes 7464960 | tf_op jit(solution)/shard_map/convert_element_type | solution.py:27
  23.8 1.9 %slice.48 = bf16[1284,1280]{1,0:T(8,128)(2,1)} slice(bf16[1312,1280]{1,0:T(8,128)(2,1)S(1)} %bitcast.178), slice={[0:1284], [0:1280]} | slice | bytes 6574080 | tf_op jit(solution)/shard_map/slice | solution.py:28
  25.9 1.9 %reshape.200 = f32[4,4,4,1284]{3,2,1,0:T(4,128)} reshape(bf16[4,4,5136]{2,1,0:T(4,128)(2,1)} %param.12) | data formatting | bytes 493056 | tf_op jit(solution)/shard_map/reshape | solution.py:86
  30.2 5.6 %collective-permute-start = (bf16[1280,2,4]{0,2,1:T(4,128)(2,1)S(1)}, bf16[1280,2,4]{0,2,1:T(4,128)(2,1)S(1)}, u32[]{:S(2)}, u32[]{:S(2)}) collective-permute-start(bf16[1280,2,4]{0,2,1:T(4,128)(2,1)S(1)} %convert_element_type.122), channel_id=1, source_target_pairs={{0,1},{1,2},{2,3},{3,4},{4,5},{5,6},{6,7},{7,8},{8,9},{9,10},{10,1... | collective-permute-start | bytes 61448 | tf_op jit(solution)/shard_map/ppermute | solution.py:36
  36.5 1.8 %reshape.201 = f32[4,1280,2,4]{1,3,2,0:T(4,128)} reshape(f32[4,16,80,2,4]{2,1,4,3,0:T(8,128)} %copy.83) | data formatting | bytes 327680 | tf_op jit(solution)/shard_map/convert_element_type | solution.py:80
  38.3 2.6 %collective-permute-start.1 = (bf16[1280,2,4]{0,2,1:T(4,128)(2,1)S(1)}, bf16[1280,2,4]{0,2,1:T(4,128)(2,1)S(1)}, u32[]{:S(2)}, u32[]{:S(2)}) collective-permute-start(bf16[1280,2,4]{0,2,1:T(4,128)(2,1)S(1)} %fusion.79), channel_id=1, source_target_pairs={{0,2},{1,3},{2,4},{3,5},{4,6},{5,7},{6,8},{7,9},{8,10},{9,11},{10,... | collective-permute-start | bytes 61448 | tf_op jit(solution)/shard_map/ppermute | solution.py:36
  42.9 3.1 %collective-permute-start.2 = (bf16[1280,2,4]{0,2,1:T(4,128)(2,1)S(1)}, bf16[1280,2,4]{0,2,1:T(4,128)(2,1)S(1)}, u32[]{:S(2)}, u32[]{:S(2)}) collective-permute-start(bf16[1280,2,4]{0,2,1:T(4,128)(2,1)S(1)} %fusion.106), channel_id=1, source_target_pairs={{0,4},{1,5},{2,6},{3,7},{4,8},{5,9},{6,10},{7,11},{8,12},{9,13},{1... | collective-permute-start | bytes 61448 | tf_op jit(solution)/shard_map/ppermute | solution.py:36
  46.2 2.1 %collective-permute-done.2 = bf16[1280,2,4]{0,2,1:T(4,128)(2,1)S(1)} collective-permute-done((bf16[1280,2,4]{0,2,1:T(4,128)(2,1)S(1)}, bf16[1280,2,4]{0,2,1:T(4,128)(2,1)S(1)}, u32[]{:S(2)}, u32[]{:S(2)}) %collective-permute-start.2) | collective-permute-done | bytes 20512 | tf_op jit(solution)/shard_map/ppermute | solution.py:36
  48.4 3.3 %collective-permute-start.3 = (bf16[1280,2,4]{0,2,1:T(4,128)(2,1)S(1)}, bf16[1280,2,4]{0,2,1:T(4,128)(2,1)S(1)}, u32[]{:S(2)}, u32[]{:S(2)}) collective-permute-start(bf16[1280,2,4]{0,2,1:T(4,128)(2,1)S(1)} %fusion.80), channel_id=1, source_target_pairs={{0,8},{1,9},{2,10},{3,11},{4,12},{5,13},{6,14},{7,15},{16,24},{17,... | collective-permute-start | bytes 61448 | tf_op jit(solution)/shard_map/ppermute | solution.py:36
  51.6 1.2 %fusion.15 = f32[4,4,4,1284]{3,0,1,2:T(4,128)S(1)} fusion(bf16[1284,1280]{1,0:T(8,128)(2,1)S(1)} %slice.49, bf16[4,4,4,1280]{3,2,1,0:T(4,128)(2,1)S(1)} %get-tuple-element.24), kind=kOutput, calls=%fused_computation.15 | convolution fusion | flops 210370560 | bytes 3779584 | tf_op jit(solution)/shard_map/lbqs,ks->lbqk/dot_general | solution.py:77
  52.9 13.7 %collective-permute-start.4 = (bf16[1280,2,4]{0,2,1:T(4,128)(2,1)S(1)}, bf16[1280,2,4]{0,2,1:T(4,128)(2,1)S(1)}, u32[]{:S(2)}, u32[]{:S(2)}) collective-permute-start(bf16[1280,2,4]{0,2,1:T(4,128)(2,1)S(1)} %add_convert_fusion.3), channel_id=1, source_target_pairs={{0,1},{1,2},{2,3},{3,4},{4,5},{5,6},{6,7},{7,8},{8,9},{9,10},{10,1... | collective-permute-start | bytes 61448 | tf_op jit(solution)/shard_map/ppermute | solution.py:41
  66.6 2.0 %fusion.28 = f32[4,4,4,1284]{3,0,1,2:T(4,128)} fusion(f32[4,4,4,1284]{3,0,1,2:T(4,128)S(1)} %fusion.15, bf16[1284,1280]{1,0:T(8,128)(2,1)S(1)} %copy-done, bf16[4,4,4,1280]{3,2,1,0:T(4,128)(2,1)S(1)} %get-tuple-element.23), kind=kOutput, calls=%fused_computation.28 | convolution fusion | flops 210534912 | bytes 4108288 | tf_op jit(solution)/shard_map/lbqs,ks->lbqk/dot_general | solution.py:76
  68.7 2.2 %reduce_window_sum.11 = f32[4,4,4,1284]{3,0,1,2:T(4,128)} reduce-window(f32[4,4,4,1284]{3,0,1,2:T(4,128)} %fusion.28, f32[]{:T(128)} %constant.88.clone.1), window={size=4x1x1x1 pad=3_0x0_0x0_0x0_0}, to_apply=%region_0.1 | reduce-window | flops 246528 | bytes 657412 | tf_op jit(solution)/shard_map/jit(cumsum)/reduce_window_sum | solution.py:82
  70.9 1.0 fusion.11
  72.7 1.0 fusion.38
  87.3 6.9 %all-to-all-start.1 = ((bf16[16,4,2,2,2,80]{5,1,4,2,3,0:T(4,128)(2,1)}), bf16[16,4,2,2,2,80]{5,1,4,2,3,0:T(4,128)(2,1)S(1)}, u32[]{:S(2)}, u32[]{:S(2)}) async-start(bf16[16,4,2,2,2,80]{5,1,4,2,3,0:T(4,128)(2,1)} %constant_dynamic-update-slice_fusion), calls=%async_computation.1 | async-start | bytes 262144 | tf_op jit(solution)/shard_map/all_to_all | solution.py:102
  94.2 6.8 %all-to-all-done.1 = bf16[16,4,2,2,2,80]{5,1,4,2,3,0:T(4,128)(2,1)S(1)} async-done(((bf16[16,4,2,2,2,80]{5,1,4,2,3,0:T(4,128)(2,1)}), bf16[16,4,2,2,2,80]{5,1,4,2,3,0:T(4,128)(2,1)S(1)}, u32[]{:S(2)}, u32[]{:S(2)}) %all-to-all-start.1) | async-done | bytes 81952 | tf_op jit(solution)/shard_map/all_to_all | solution.py:102
  101.4 4.1 %fusion.4 = bf16[4,80,2,2,1280]{4,0,3,1,2:T(4,128)(2,1)S(1)} fusion(bf16[4,2,2,32,80]{3,0,1,4,2:T(4,128)(2,1)S(1)} %copy.109, bf16[80,32,1280]{2,1,0:T(8,128)(2,1)} %param.10), kind=kOutput, calls=%fused_computation.6 | convolution fusion | flops 104857600 | bytes 9912320 | tf_op jit(solution)/shard_map/lcehs,shj->lsecj/dot_general | solution.py:104
  105.6 1.6 %fusion.21 = bf16[4,80,2,1280]{3,0,2,1:T(4,128)(2,1)S(1)} fusion(bf16[4,80,2,2,1280]{4,0,3,1,2:T(4,128)(2,1)S(1)} %fusion.4, pred[1280]{0:T(1024)(128)(4,1)S(1)} %fusion.97, pred[80,1280]{1,0:T(8,128)(4,1)S(1)} %copy-done.3), kind=kLoop, calls=%fused_computation.22 | loop fusion | flops 1638400 | bytes 5018880 | tf_op jit(solution)/shard_map/convert_element_type | solution.py:106
  107.2 2.4 %copy.100 = bf16[4,80,2,1280]{3,2,1,0:T(2,128)(2,1)} copy(bf16[4,80,2,1280]{3,0,2,1:T(4,128)(2,1)S(1)} %fusion.21) | data formatting | bytes 3276800 | tf_op jit(solution)/shard_map/convert_element_type | solution.py:106
  (87 shorter events, 23.6 us)
Async XLA Ops:
  0.9 0.6 copy-start.2
  5.1 6.5 %copy-start.10 = (f32[32]{0:T(128)S(1)}, f32[32]{0:T(128)}, u32[]{:S(2)}) copy-start(f32[32]{0:T(128)} %param.11) | copy-start | bytes 388
  5.1 14.3 %copy-start.7 = (s32[1280]{0:T(1024)S(1)}, s32[1280]{0:T(1024)}, u32[]{:S(2)}) copy-start(s32[1280]{0:T(1024)} %param.9) | copy-start | bytes 15364
  12.6 15.9 %all-to-all-start = ((bf16[4,80,2,64]{1,2,0,3:T(2,128)(2,1)}), bf16[4,80,2,64]{1,2,0,3:T(2,128)(2,1)S(1)}, u32[]{:S(2)}, u32[]{:S(2)}) async-start(bf16[4,80,2,64]{1,2,0,3:T(2,128)(2,1)} %copy.81), calls=%async_computation | async-start | bytes 262144 | tf_op jit(solution)/shard_map/all_to_all | solution.py:62
  21.2 2.5 %copy-start.8 = (s32[4,4,4]{2,1,0:T(4,128)S(1)}, s32[4,4,4]{2,1,0:T(4,128)}, u32[]{:S(2)}) copy-start(s32[4,4,4]{2,1,0:T(4,128)} %param.13) | copy-start | bytes 772
  30.2 8.2 %collective-permute-start = (bf16[1280,2,4]{0,2,1:T(4,128)(2,1)S(1)}, bf16[1280,2,4]{0,2,1:T(4,128)(2,1)S(1)}, u32[]{:S(2)}, u32[]{:S(2)}) collective-permute-start(bf16[1280,2,4]{0,2,1:T(4,128)(2,1)S(1)} %convert_element_type.122), channel_id=1, source_target_pairs={{0,1},{1,2},{2,3},{3,4},{4,5},{5,6},{6,7},{7,8},{8,9},{9,10},{10,1... | collective-permute-start | bytes 61448 | tf_op jit(solution)/shard_map/ppermute | solution.py:36
  38.3 4.5 %collective-permute-start.1 = (bf16[1280,2,4]{0,2,1:T(4,128)(2,1)S(1)}, bf16[1280,2,4]{0,2,1:T(4,128)(2,1)S(1)}, u32[]{:S(2)}, u32[]{:S(2)}) collective-permute-start(bf16[1280,2,4]{0,2,1:T(4,128)(2,1)S(1)} %fusion.79), channel_id=1, source_target_pairs={{0,2},{1,3},{2,4},{3,5},{4,6},{5,7},{6,8},{7,9},{8,10},{9,11},{10,... | collective-permute-start | bytes 61448 | tf_op jit(solution)/shard_map/ppermute | solution.py:36
  42.9 5.4 %collective-permute-start.2 = (bf16[1280,2,4]{0,2,1:T(4,128)(2,1)S(1)}, bf16[1280,2,4]{0,2,1:T(4,128)(2,1)S(1)}, u32[]{:S(2)}, u32[]{:S(2)}) collective-permute-start(bf16[1280,2,4]{0,2,1:T(4,128)(2,1)S(1)} %fusion.106), channel_id=1, source_target_pairs={{0,4},{1,5},{2,6},{3,7},{4,8},{5,9},{6,10},{7,11},{8,12},{9,13},{1... | collective-permute-start | bytes 61448 | tf_op jit(solution)/shard_map/ppermute | solution.py:36
  46.2 20.4 %copy-start = (bf16[1284,1280]{1,0:T(8,128)(2,1)S(1)}, bf16[1284,1280]{1,0:T(8,128)(2,1)}, u32[]{:S(2)}) copy-start(bf16[1284,1280]{1,0:T(8,128)(2,1)} %slice.48) | copy-start | bytes 9861124
  48.4 4.5 %collective-permute-start.3 = (bf16[1280,2,4]{0,2,1:T(4,128)(2,1)S(1)}, bf16[1280,2,4]{0,2,1:T(4,128)(2,1)S(1)}, u32[]{:S(2)}, u32[]{:S(2)}) collective-permute-start(bf16[1280,2,4]{0,2,1:T(4,128)(2,1)S(1)} %fusion.80), channel_id=1, source_target_pairs={{0,8},{1,9},{2,10},{3,11},{4,12},{5,13},{6,14},{7,15},{16,24},{17,... | collective-permute-start | bytes 61448 | tf_op jit(solution)/shard_map/ppermute | solution.py:36
  52.9 17.9 %collective-permute-start.4 = (bf16[1280,2,4]{0,2,1:T(4,128)(2,1)S(1)}, bf16[1280,2,4]{0,2,1:T(4,128)(2,1)S(1)}, u32[]{:S(2)}, u32[]{:S(2)}) collective-permute-start(bf16[1280,2,4]{0,2,1:T(4,128)(2,1)S(1)} %add_convert_fusion.3), channel_id=1, source_target_pairs={{0,1},{1,2},{2,3},{3,4},{4,5},{5,6},{6,7},{7,8},{8,9},{9,10},{10,1... | collective-permute-start | bytes 61448 | tf_op jit(solution)/shard_map/ppermute | solution.py:41
  70.8 1.9 %copy-start.1 = (bf16[1284,1280]{1,0:T(8,128)(2,1)S(1)}, bf16[1284,1280]{1,0:T(8,128)(2,1)}, u32[]{:S(2)}) copy-start(bf16[1284,1280]{1,0:T(8,128)(2,1)} %slice.48) | copy-start | bytes 9861124
  70.8 3.0 %copy-start.4 = (f32[4,4,4,1284]{3,2,1,0:T(4,128)S(1)}, f32[4,4,4,1284]{3,2,1,0:T(4,128)}, u32[]{:S(2)}) copy-start(f32[4,4,4,1284]{3,2,1,0:T(4,128)} %reshape.200) | copy-start | bytes 986116
  70.9 3.0 %copy-start.5 = (f32[4,4,4,1284]{3,0,1,2:T(4,128)S(1)}, f32[4,4,4,1284]{3,0,1,2:T(4,128)}, u32[]{:S(2)}) copy-start(f32[4,4,4,1284]{3,0,1,2:T(4,128)} %fusion.28) | copy-start | bytes 986116
  70.9 3.0 %copy-start.6 = (f32[4,4,4,1284]{3,0,1,2:T(4,128)S(1)}, f32[4,4,4,1284]{3,0,1,2:T(4,128)}, u32[]{:S(2)}) copy-start(f32[4,4,4,1284]{3,0,1,2:T(4,128)} %reduce_window_sum.11) | copy-start | bytes 986116
  70.9 3.0 %copy-start.9 = (f32[4,4,4]{0,2,1:T(4,128)S(1)}, f32[4,4,4]{0,2,1:T(4,128)}, u32[]{:S(2)}) copy-start(f32[4,4,4]{0,2,1:T(4,128)} %copy.76) | copy-start | bytes 772
  70.9 3.0 %copy-start.11 = (f32[4]{0:T(128)S(1)}, f32[4]{0:T(128)}, u32[]{:S(2)}) copy-start(f32[4]{0:T(128)} %param.15) | copy-start | bytes 52
  70.9 3.0 %copy-start.12 = (s32[1,4]{1,0:T(1,128)S(1)}, s32[1,4]{1,0:T(1,128)}, u32[]{:S(2)}) copy-start(s32[1,4]{1,0:T(1,128)} %param.14) | copy-start | bytes 52
  87.3 13.8 %all-to-all-start.1 = ((bf16[16,4,2,2,2,80]{5,1,4,2,3,0:T(4,128)(2,1)}), bf16[16,4,2,2,2,80]{5,1,4,2,3,0:T(4,128)(2,1)S(1)}, u32[]{:S(2)}, u32[]{:S(2)}) async-start(bf16[16,4,2,2,2,80]{5,1,4,2,3,0:T(4,128)(2,1)} %constant_dynamic-update-slice_fusion), calls=%async_computation.1 | async-start | bytes 262144 | tf_op jit(solution)/shard_map/all_to_all | solution.py:102
  101.4 4.2 %copy-start.3 = (pred[80,1280]{1,0:T(8,128)(4,1)S(1)}, pred[80,1280]{1,0:T(8,128)(4,1)}, u32[]{:S(2)}) copy-start(pred[80,1280]{1,0:T(8,128)(4,1)} %copy-done.2) | copy-start | bytes 307204
